TPU v7x, 512 devices: a whole 4x8x8 slice. The times are simulated.
512 devices in a mesh: seq: 128 (over z, y, core), tp: 4 (over x).
Axes of the slice: x: 4, y: 8, z: 8, core: 2. Of those that a mesh axis runs over, the one named last changes fastest.
Arguments:
- queries: bfloat16 [32768, 4096], P('seq', 'tp'), may hold values from -6 to 6, as said below
- keys: bfloat16 [32768, 512], P('seq', 'tp'), may hold values from -6 to 6, as said below
- values: bfloat16 [32768, 512], P('seq', 'tp'), may hold values from -6 to 6
- segment: int32 [32768], P('seq'), may hold values from 0 to 255, never falling along the last dimension, each value on 1 to 512 neighbouring positions
- repack: int32 [32768], P('seq'), may hold values from 0 to 32767, as said below
- proj: bfloat16 [1536, 4096], P('seq', 'tp'), may hold values from -0.5 to 0.5
- student_states: bfloat16 [32768, 1536], P('seq'), may hold values from -6 to 6
- target_row: int32 [32768], P('seq'), may hold values from 0 to 255
Outputs:
- student_rows: bfloat16 [32768, 1536], P('seq', 'tp')
- grad: float32 [1536, 4096], P('seq', 'tp')
Inputs may be any that keep to these rules, and one draw needn't show every extreme that they name: `queries`: scaled normal entries. `keys`: scaled normal entries. `repack`: A permutation of the student rows. Each device's teacher rows go in consecutive groups of 4 rows, in order, each group to one student owner (the device holding student rows owner * 256 to owner * 256 + 255); every device sends exactly 4 rows to each of 64 other devices and none to itself, so at most 4 rows from one device to one owner, reached by every sending pair.
All inputs are finite; a program needn't handle non-finite values.
Results may differ from a plain program's by a relative error of at most 0.0056.
Values may be sent and summed in bfloat16 or wider, within the bound.
No kernel may reach another device: no remote copies, remote signals or barrier semaphores. Data moves between devices by JAX's collectives and lax.ppermute only.
A program may use at most 64 MiB of HBM per device.

v0:
```python
import math
import jax
import jax.numpy as jnp
from jax import lax
from jax.sharding import PartitionSpec as P

HEADS = 32
KV_HEADS = 4
HEAD_DIM = 128
SW = 1536
REACH = 2
neg_large = -1e30


def prefix(value, axis, combine, identity):
    size, here = (lax.axis_size(axis), lax.axis_index(axis))
    everything = jax.tree.map(lambda part: lax.all_gather(part, axis), value)
    start = jax.tree.map(
        lambda part, zero: jnp.broadcast_to(jnp.asarray(zero, part.dtype), part.shape),
        value,
        identity,
    )

    def hop(k, before):
        reached = k < here
        new = combine(before, jax.tree.map(lambda part: part[k], everything))
        return jax.tree.map(lambda a, b: jnp.where(reached, a, b), new, before)

    return lax.fori_loop(0, size, hop, start)


def passed_along(block, axis, distance):
    devices = range(lax.axis_size(axis))
    route = [(i - distance, i) for i in devices if i - distance in devices]
    return lax.ppermute(block, axis, route)


def anchor_combine(earlier, later):
    first_id = jnp.where(earlier[0] < 0, later[0], earlier[0])
    last_id = jnp.where(later[1] < 0, earlier[1], later[1])
    whole_later = (later[0] == later[1]) & (later[0] == earlier[1]) & (later[0] >= 0)
    start_pos = jnp.where(later[1] < 0, earlier[2], jnp.where(whole_later, earlier[2], later[2]))
    return (first_id, last_id, start_pos)


def document_starts(segment):
    row_count = segment.shape[0]
    row_pos = lax.axis_index("seq") * row_count + jnp.arange(row_count, dtype=jnp.int32)
    first_id = segment[0]
    last_id = segment[-1]
    last_start = jnp.min(jnp.where(segment == last_id, row_pos, jnp.int32(2**30)))
    sentinel = jnp.int32(-1)
    carried = prefix(
        (first_id, last_id, last_start), "seq", anchor_combine, (sentinel, sentinel, sentinel)
    )
    is_new = jnp.concatenate([jnp.ones((1,), bool), segment[1:] != segment[:-1]])
    local_start = lax.cummax(jnp.where(is_new, row_pos, jnp.int32(-1)), axis=0)
    inherit = (segment == carried[1]) & (segment == first_id)
    return (jnp.where(inherit, carried[2], local_start), row_pos)


def attend(queries, keys, values, row_start, row_pos):
    row_count = queries.shape[0]
    key_list = [keys]
    value_list = [values]
    pos_list = [row_pos]
    for step in range(1, REACH + 1):
        earlier = passed_along((keys, values), "seq", step)
        key_list.insert(0, earlier[0])
        value_list.insert(0, earlier[1])
        pos_list.insert(0, row_pos - step * row_count)
    all_keys = jnp.concatenate(key_list, axis=0)
    all_values = jnp.concatenate(value_list, axis=0)
    key_pos = jnp.concatenate(pos_list, axis=0)
    allowed = (key_pos[None, :] >= row_start[:, None]) & (key_pos[None, :] <= row_pos[:, None])
    kv_local = keys.shape[1] // HEAD_DIM
    group = HEADS // KV_HEADS
    part_size = 1
    q_heads = queries.reshape(row_count, kv_local, group, HEAD_DIM)
    scale = 1.0 / math.sqrt(HEAD_DIM)
    outputs = []
    for first in range(0, group, part_size):
        q_part = q_heads[:, 0, first : first + part_size, :]
        scores = (
            jnp.einsum("tjd,sd->jts", q_part, all_keys, preferred_element_type=jnp.float32) * scale
        )
        scores = jnp.where(allowed[None], scores, neg_large)
        top = jnp.max(scores, axis=-1, keepdims=True)
        expo = jnp.exp(scores - top)
        weights = (expo / jnp.sum(expo, axis=-1, keepdims=True)).astype(jnp.bfloat16)
        mixed = jnp.einsum("jts,sd->tjd", weights, all_values, preferred_element_type=jnp.float32)
        outputs.append(mixed.astype(jnp.bfloat16))
    return jnp.concatenate(outputs, axis=1).reshape(row_count, -1)


def project_rows(row_data, proj):
    return jnp.einsum(
        "tf,nf->tn",
        row_data,
        lax.all_gather(proj, "seq", axis=0, tiled=True),
        preferred_element_type=jnp.float32,
    )


def fill_buckets(data, target_dev, slot_rank, devices, capacity):
    empty = jnp.zeros((devices, capacity, data.shape[1]), data.dtype)
    return empty.at[target_dev, slot_rank].set(data)


def place_rows(received, slots, row_count):
    width = received.shape[-1]
    holder = jnp.zeros((row_count + 1, width), received.dtype)
    holder = holder.at[slots.reshape(-1)].set(received.reshape(-1, width))
    return holder[:row_count]


def on_device(queries, keys, values, segment, repack, proj, student_states, target_row):
    row_count = queries.shape[0]
    devices = lax.axis_size("seq")
    row_start, row_pos = document_starts(segment)
    attended = attend(queries, keys, values, row_start, row_pos)
    capacity = max(2 * row_count // devices, 2)
    target_dev = repack // row_count
    local_slot = repack - target_dev * row_count
    same_dev = target_dev[:, None] == target_dev[None, :]
    row_ids = jnp.arange(row_count, dtype=jnp.int32)
    before = row_ids[None, :] < row_ids[:, None]
    slot_rank = jnp.sum((same_dev & before).astype(jnp.int32), axis=1)
    slot_table = (
        jnp.full((devices, capacity), row_count, jnp.int32)
        .at[target_dev, slot_rank]
        .set(local_slot)
    )
    width_share = SW // lax.axis_size("tp")
    tp_index = lax.axis_index("tp")
    targets = student_states[target_row]
    buckets = fill_buckets(attended, target_dev, slot_rank, devices, capacity)
    arrived = (
        lax.all_to_all(buckets, "seq", split_axis=0, concat_axis=0, tiled=True),
        lax.all_to_all(slot_table, "seq", split_axis=0, concat_axis=0, tiled=True),
    )
    student_x = place_rows(arrived[0], arrived[1], row_count)
    y_part = project_rows(student_x, proj)
    y_total = lax.psum(y_part, "tp")
    y_rounded = y_total.astype(jnp.bfloat16)
    delta = (y_rounded.astype(jnp.float32) - targets.astype(jnp.float32)).astype(jnp.bfloat16)
    out_rows = lax.dynamic_slice_in_dim(y_rounded, tp_index * width_share, width_share, 1)
    norm_factor = 1.0 / math.sqrt(row_count * devices)
    grad_rows = delta.shape[1] // devices
    term = jnp.einsum("ts,tf->sf", delta, student_x, preferred_element_type=jnp.float32)
    pieces = term.reshape(devices, grad_rows, term.shape[1])
    summed = lax.all_to_all(
        pieces.astype(jnp.bfloat16), "seq", split_axis=0, concat_axis=0, tiled=True
    ).astype(pieces.dtype)
    grad = jnp.sum(summed, axis=0) * norm_factor
    return (out_rows, grad)


def solution(mesh):
    placed = (
        P("seq", "tp"),
        P("seq", "tp"),
        P("seq", "tp"),
        P("seq"),
        P("seq"),
        P("seq", "tp"),
        P("seq", None),
        P("seq"),
    )
    return jax.shard_map(
        on_device,
        mesh=mesh,
        in_specs=placed,
        out_specs=(P("seq", "tp"), P("seq", "tp")),
        check_vma=False,
    )
```

profile of v0, /device:TPU:41, one launch (start us, length us, event | category | flops | bytes accessed | tf_op | source)
XLA Modules:
  0.0 1131.9 jit_solution(2342865572813222749)
XLA Ops:
  7.2 2.4 collective-permute-start
  9.7 3.1 collective-permute-start.1
  12.8 3.2 collective-permute-start.2
  16.1 2.2 collective-permute-start.3
  18.3 0.7 multiply_subtract_fusion
  19.2 11.1 scatter_fusion
  30.3 0.7 copy.34
  31.0 15.8 %all-to-all-start = ((s32[128,1,4]{2,1,0:T(1,128)}), s32[128,1,4]{2,1,0:T(1,128)S(1)}, u32[]{:S(2)}, u32[]{:S(2)}) async-start(s32[128,1,4]{2,1,0:T(1,128)} %copy.34), calls=%async_computation | async-start | bytes 131072 | tf_op jit(solution)/shard_map/all_to_all | solution.py:140
  46.9 1.2 copy.35
  48.9 1.3 dynamic-slice
  50.1 1.2 fusion.59
  52.0 1.3 fusion.56
  53.3 1.3 dynamic-update-slice.2
  54.6 18.9 %all-reduce.3 = (s32[128]{0:T(128)S(1)}, s32[128]{0:T(128)S(1)}, s32[128]{0:T(128)S(1)}) all-reduce(s32[128]{0:T(128)S(1)} %get-tuple-element.149, s32[128]{0:T(128)S(1)} %slice_dynamic-update-slice_fusion, s32[128]{0:T(128)S(1)} %dynamic-update-slice.2), channel_id=1, replica_groups=mesh['seq'=128,'tp'=4] {'seq'}, use_global_device_ids=true, to_apply=%add | all-reduce | flops 384 | bytes 3072
  73.5 786.0 %while.15 = (s32[]{:T(128)}, s32[]{:T(128)}, s32[]{:T(128)}, s32[]{:T(128)}, s32[128]{0:T(128)S(1)}, /*index=5*/s32[128]{0:T(128)S(1)}, s32[128]{0:T(128)S(1)}, s32[]{:T(128)}, s32[]{:T(128)}) while((s32[]{:T(128)}, s32[]{:T(128)}, s32[]{:T(128)}, s32[]{:T(128)}, s32[128]{0:T(128)S(1)}, /*index=5*/s32[128]{0:T(128)S(1)}, s32[128]{0:T(128)S(1)}, ...), condition=%wide.region_4.5_spmd, body=%wide.region_3.4_spmd.sunk | while | flops 14 | bytes 261 | solution.py:29
  859.6 0.7 and_select_fusion
  866.9 1.2 broadcast_in_dim.35
  868.1 36.8 %scatter_fusion.1 = bf16[128,4,1024]{2,1,0:T(4,128)(2,1)} fusion(bf16[128,4,1024]{2,1,0:T(4,128)(2,1)} %broadcast_in_dim.35, s32[256]{0:T(256)S(1)} %bitcast.214, bf16[256,1024]{1,0:T(8,128)(2,1)S(1)} %copy.44), kind=kCustom, calls=%fused_computation.2 | custom fusion | bytes 1574912 | tf_op jit(solution)/shard_map/scatter | solution.py:107
  904.9 15.5 %all-to-all-start.1 = ((bf16[128,4,1024]{2,1,0:T(4,128)(2,1)}), bf16[128,4,1024]{2,1,0:T(4,128)(2,1)S(1)}, u32[]{:S(2)}, u32[]{:S(2)}) async-start(bf16[128,4,1024]{2,1,0:T(4,128)(2,1)} %scatter_fusion.1), calls=%async_computation.1 | async-start | bytes 2097152 | tf_op jit(solution)/shard_map/all_to_all | solution.py:139
  920.5 2.1 gather_fusion
  923.1 0.8 reduce.21
  924.1 25.2 %all-to-all-done.1 = bf16[128,4,1024]{2,1,0:T(4,128)(2,1)S(1)} async-done(((bf16[128,4,1024]{2,1,0:T(4,128)(2,1)}), bf16[128,4,1024]{2,1,0:T(4,128)(2,1)S(1)}, u32[]{:S(2)}, u32[]{:S(2)}) %all-to-all-start.1) | async-done | bytes 1048608 | tf_op jit(solution)/shard_map/all_to_all | solution.py:139
  949.5 2.8 scatter_custom_fusion.2
  952.3 6.2 reshape.408
  958.5 2.9 fusion.41
  961.4 34.9 %all-reduce.5 = bf16[256,1536]{1,0:T(8,128)(2,1)} all-reduce(f32[256,1536]{1,0:T(8,128)S(1)} %fusion.41), channel_id=1, replica_groups=mesh['seq'=128,'tp'=4] {'tp'}, use_global_device_ids=true, to_apply=%region_25.26 | all-reduce | flops 393216 | bytes 2359296 | tf_op jit(solution)/shard_map/psum | solution.py:144
  996.3 4.1 convolution_convert_fusion
  1000.4 6.1 convert_element_type.158
  1006.4 11.2 all-to-all-start.2
  1017.7 1.6 constant_dynamic-slice_fusion
  1019.3 102.1 %all-to-all-done.2 = bf16[128,12,1024]{2,1,0:T(8,128)(2,1)} async-done(((bf16[128,12,1024]{2,1,0:T(8,128)(2,1)}), bf16[128,12,1024]{2,1,0:T(8,128)(2,1)}, u32[]{:S(2)}, u32[]{:S(2)}) %all-to-all-start.2) | async-done | bytes 3145760 | tf_op jit(solution)/shard_map/all_to_all | solution.py:152
  1121.4 3.0 convert_reduce_fusion
  (457 shorter events, 242.0 us)
Async XLA Ops:
  7.2 913.3 %copy-start = (bf16[256,1536]{1,0:T(8,128)(2,1)S(1)}, bf16[256,1536]{1,0:T(8,128)(2,1)}, u32[]{:S(2)}) copy-start(bf16[256,1536]{1,0:T(8,128)(2,1)} %param.16) | copy-start | bytes 2359300
  7.2 853.1 %copy-start.1 = (bf16[256,128]{1,0:T(8,128)(2,1)S(1)}, bf16[256,128]{1,0:T(8,128)(2,1)}, u32[]{:S(2)}) copy-start(bf16[256,128]{1,0:T(8,128)(2,1)} %param.11) | copy-start | bytes 196612
  7.2 41.0 %copy-start.3 = (s32[256]{0:T(256)S(1)}, s32[256]{0:T(256)}, u32[]{:S(2)}) copy-start(s32[256]{0:T(256)} %param.13) | copy-start | bytes 3076
  7.2 945.1 %all-gather.3.cloned.1.call-start = ((), (), s32[]{:S(2)}) async-start(), calls=%async_computation.3 | async-start | bytes 4227072 | tf_op jit(solution)/shard_map/all_gather | solution.py:100
  7.2 854.4 %collective-permute-start = (bf16[256,128]{1,0:T(8,128)(2,1)}, bf16[256,128]{1,0:T(8,128)(2,1)S(1)}, u32[]{:S(2)}, u32[]{:S(2)}) collective-permute-start(bf16[256,128]{1,0:T(8,128)(2,1)} %param.12), channel_id=1, source_target_pairs={{0,8},{4,12},{8,16},{12,20},{16,24},{20,28},{24,32},{28,36},{32,40... | collective-permute-start | bytes 196616 | tf_op jit(solution)/shard_map/ppermute | solution.py:35
  9.7 852.0 %collective-permute-start.1 = (bf16[256,128]{1,0:T(8,128)(2,1)}, bf16[256,128]{1,0:T(8,128)(2,1)S(1)}, u32[]{:S(2)}, u32[]{:S(2)}) collective-permute-start(bf16[256,128]{1,0:T(8,128)(2,1)} %param.12), channel_id=1, source_target_pairs={{0,4},{4,8},{8,12},{12,16},{16,20},{20,24},{24,28},{28,32},{32,36}... | collective-permute-start | bytes 196616 | tf_op jit(solution)/shard_map/ppermute | solution.py:35
  12.8 847.4 %collective-permute-start.2 = (bf16[256,128]{1,0:T(8,128)(2,1)}, bf16[256,128]{1,0:T(8,128)(2,1)S(1)}, u32[]{:S(2)}, u32[]{:S(2)}) collective-permute-start(bf16[256,128]{1,0:T(8,128)(2,1)} %param.11), channel_id=1, source_target_pairs={{0,8},{4,12},{8,16},{12,20},{16,24},{20,28},{24,32},{28,36},{32,40... | collective-permute-start | bytes 196616 | tf_op jit(solution)/shard_map/ppermute | solution.py:35
  16.1 844.2 %collective-permute-start.3 = (bf16[256,128]{1,0:T(8,128)(2,1)}, bf16[256,128]{1,0:T(8,128)(2,1)S(1)}, u32[]{:S(2)}, u32[]{:S(2)}) collective-permute-start(bf16[256,128]{1,0:T(8,128)(2,1)} %param.11), channel_id=1, source_target_pairs={{0,4},{4,8},{8,12},{12,16},{16,20},{20,24},{24,28},{28,32},{32,36}... | collective-permute-start | bytes 196616 | tf_op jit(solution)/shard_map/ppermute | solution.py:35
  31.0 873.9 %all-to-all-start = ((s32[128,1,4]{2,1,0:T(1,128)}), s32[128,1,4]{2,1,0:T(1,128)S(1)}, u32[]{:S(2)}, u32[]{:S(2)}) async-start(s32[128,1,4]{2,1,0:T(1,128)} %copy.34), calls=%async_computation | async-start | bytes 131072 | tf_op jit(solution)/shard_map/all_to_all | solution.py:140
  860.3 1.4 copy-start.2
  868.1 52.3 %copy-start.4 = (s32[256]{0:T(256)S(1)}, s32[256]{0:T(256)}, u32[]{:S(2)}) copy-start(s32[256]{0:T(256)} %param.17) | copy-start | bytes 3076
  904.9 44.3 %all-to-all-start.1 = ((bf16[128,4,1024]{2,1,0:T(4,128)(2,1)}), bf16[128,4,1024]{2,1,0:T(4,128)(2,1)S(1)}, u32[]{:S(2)}, u32[]{:S(2)}) async-start(bf16[128,4,1024]{2,1,0:T(4,128)(2,1)} %scatter_fusion.1), calls=%async_computation.1 | async-start | bytes 2097152 | tf_op jit(solution)/shard_map/all_to_all | solution.py:139
  1006.4 114.9 %all-to-all-start.2 = ((bf16[128,12,1024]{2,1,0:T(8,128)(2,1)}), bf16[128,12,1024]{2,1,0:T(8,128)(2,1)}, u32[]{:S(2)}, u32[]{:S(2)}) async-start(bf16[128,12,1024]{2,1,0:T(8,128)(2,1)} %convert_element_type.158), calls=%async_computation.2 | async-start | bytes 8388608 | tf_op jit(solution)/shard_map/all_to_all | solution.py:152
Sparse Core Ops, SparseCore 0:
  18.4 86.5 all-gather.2
where the time goes:
time: 1140 us; the launch traced here: 1130 us
  loops' own time  554 us (49%)
  local copies, waits for them, and re-layouts  308 us (27%)
  waiting for transfers between devices  127 us (11%)
  blocking collectives  53.8 us (5%)
  starting transfers between devices  53.6 us (5%)
  between operations  14.4 us (1%)
  matrix products  11.8 us (1%)
    another operation x1, loops' own time, prefix(): return lax.fori_loop(0, size, hop, start)  554 us
    dynamic_slice x384, local copies, waits for them, and re-layouts, hop(): new = combine(before, jax.tree.map(lambda part: part[k], everything))  232 us
    all_to_all x1, waiting for transfers between devices, on_device(): lax.all_to_all(pieces.astype(jnp.bfloat16), 'seq', split_axis=0, concat_a...  102 us
    scatter x1, local copies, waits for them, and re-layouts, fill_buckets(): return empty.at[target_dev, slot_rank].set(data)  36.8 us
    psum x1, blocking collectives, on_device(): y_total = lax.psum(y_part, 'tp')  34.9 us
    all_to_all x1, waiting for transfers between devices, on_device(): lax.all_to_all(buckets, 'seq', split_axis=0, concat_axis=0, tiled=True)  25.2 us
  transfers between devices with their start and end apart: 8, of which 2 were waited for; matrix products, arithmetic and copies ran while one was open for 27% of the time, Pallas kernels for 0%

commit v1 on v0

--- a/solution.py
+++ b/solution.py
@@ -141,7 +141,9 @@
     )
     student_x = place_rows(arrived[0], arrived[1], row_count)
     y_part = project_rows(student_x, proj)
-    y_total = lax.psum(y_part, "tp")
+    y_total = y_part
+    for hop_ in (1, 2):
+        y_total = y_total + lax.ppermute(y_total, "tp", [(dev, dev ^ hop_) for dev in range(4)])
     y_rounded = y_total.astype(jnp.bfloat16)
     delta = (y_rounded.astype(jnp.float32) - targets.astype(jnp.float32)).astype(jnp.bfloat16)
     out_rows = lax.dynamic_slice_in_dim(y_rounded, tp_index * width_share, width_share, 1)

time: 1140 us -> 1180 us (1.035)
  the two profiles are of different devices: /device:TPU:41 before, /device:TPU:33 now
where the time goes in v1:
time: 1180 us; the launch traced here: 1170 us
  loops' own time  554 us (47%)
  local copies, waits for them, and re-layouts  309 us (26%)
  waiting for transfers between devices  192 us (16%)
  starting transfers between devices  62.5 us (5%)
  blocking collectives  19 us (2%)
  between operations  14.5 us (1%)
    another operation x1, loops' own time, prefix(): return lax.fori_loop(0, size, hop, start)  554 us
    dynamic_slice x384, local copies, waits for them, and re-layouts, hop(): new = combine(before, jax.tree.map(lambda part: part[k], everything))  232 us
    all_to_all x1, waiting for transfers between devices, on_device(): lax.all_to_all(pieces.astype(jnp.bfloat16), 'seq', split_axis=0, concat_a...  101 us
    ppermute x2, waiting for transfers between devices, on_device(): lax.ppermute(y_total, 'tp', [(dev, dev ^ hop_) for dev in range(4)])  65.3 us
    scatter x1, local copies, waits for them, and re-layouts, fill_buckets(): return empty.at[target_dev, slot_rank].set(data)  36.6 us
    all_to_all x1, waiting for transfers between devices, on_device(): lax.all_to_all(buckets, 'seq', split_axis=0, concat_axis=0, tiled=True)  26.4 us
  transfers between devices with their start and end apart: 10, of which 4 were waited for; matrix products, arithmetic and copies ran while one was open for 26% of the time, Pallas kernels for 0%

profile of v1, /device:TPU:33, one launch (start us, length us, event | category | flops | bytes accessed | tf_op | source)
XLA Modules:
  0.0 1172.5 jit_solution(17641855486841315615)
XLA Ops:
  7.2 2.4 collective-permute-start
  9.7 3.1 collective-permute-start.1
  12.8 2.3 collective-permute-start.2
  15.2 2.2 collective-permute-start.3
  18.3 11.1 scatter_fusion
  30.1 16.8 %all-to-all-start = ((s32[128,1,4]{2,1,0:T(1,128)}), s32[128,1,4]{2,1,0:T(1,128)S(1)}, u32[]{:S(2)}, u32[]{:S(2)}) async-start(s32[128,1,4]{2,1,0:T(1,128)} %copy.34), calls=%async_computation | async-start | bytes 131072 | tf_op jit(solution)/shard_map/all_to_all | solution.py:140
  47.0 1.2 copy.35
  49.0 1.3 dynamic-slice
  50.2 1.2 fusion.59
  52.1 1.3 fusion.56
  53.4 1.3 dynamic-update-slice.2
  54.7 19.0 %all-reduce.3 = (s32[128]{0:T(128)S(1)}, s32[128]{0:T(128)S(1)}, s32[128]{0:T(128)S(1)}) all-reduce(s32[128]{0:T(128)S(1)} %get-tuple-element.149, s32[128]{0:T(128)S(1)} %slice_dynamic-update-slice_fusion, s32[128]{0:T(128)S(1)} %dynamic-update-slice.2), channel_id=1, replica_groups=mesh['seq'=128,'tp'=4] {'seq'}, use_global_device_ids=true, to_apply=%add | all-reduce | flops 384 | bytes 3072
  73.7 786.0 %while.15 = (s32[]{:T(128)}, s32[]{:T(128)}, s32[]{:T(128)}, s32[]{:T(128)}, s32[128]{0:T(128)S(1)}, /*index=5*/s32[128]{0:T(128)S(1)}, s32[128]{0:T(128)S(1)}, s32[]{:T(128)}, s32[]{:T(128)}) while((s32[]{:T(128)}, s32[]{:T(128)}, s32[]{:T(128)}, s32[]{:T(128)}, s32[128]{0:T(128)S(1)}, /*index=5*/s32[128]{0:T(128)S(1)}, s32[128]{0:T(128)S(1)}, ...), condition=%wide.region_4.5_spmd, body=%wide.region_3.4_spmd.sunk | while | flops 14 | bytes 261 | solution.py:29
  867.1 1.2 broadcast_in_dim.35
  868.4 36.6 %scatter_fusion.1 = bf16[128,4,1024]{2,1,0:T(4,128)(2,1)} fusion(bf16[128,4,1024]{2,1,0:T(4,128)(2,1)} %broadcast_in_dim.35, s32[256]{0:T(256)S(1)} %bitcast.214, bf16[256,1024]{1,0:T(8,128)(2,1)S(1)} %copy.44), kind=kCustom, calls=%fused_computation.2 | custom fusion | bytes 1574912 | tf_op jit(solution)/shard_map/scatter | solution.py:107
  904.9 15.6 %all-to-all-start.1 = ((bf16[128,4,1024]{2,1,0:T(4,128)(2,1)}), bf16[128,4,1024]{2,1,0:T(4,128)(2,1)S(1)}, u32[]{:S(2)}, u32[]{:S(2)}) async-start(bf16[128,4,1024]{2,1,0:T(4,128)(2,1)} %scatter_fusion.1), calls=%async_computation.1 | async-start | bytes 2097152 | tf_op jit(solution)/shard_map/all_to_all | solution.py:139
  922.0 26.4 %all-to-all-done.1 = bf16[128,4,1024]{2,1,0:T(4,128)(2,1)S(1)} async-done(((bf16[128,4,1024]{2,1,0:T(4,128)(2,1)}), bf16[128,4,1024]{2,1,0:T(4,128)(2,1)S(1)}, u32[]{:S(2)}, u32[]{:S(2)}) %all-to-all-start.1) | async-done | bytes 1048608 | tf_op jit(solution)/shard_map/all_to_all | solution.py:139
  948.7 2.8 scatter_custom_fusion.2
  951.5 6.2 reshape.408
  957.7 2.9 fusion.41
  960.6 3.1 collective-permute-start.4
  963.7 34.2 %collective-permute-done.4 = f32[256,1536]{1,0:T(8,128)S(1)} collective-permute-done((f32[256,1536]{1,0:T(8,128)S(1)}, f32[256,1536]{1,0:T(8,128)S(1)}, u32[]{:S(2)}, u32[]{:S(2)}) %collective-permute-start.4) | collective-permute-done | bytes 1572896 | tf_op jit(solution)/shard_map/ppermute | solution.py:146
  998.1 4.6 collective-permute-start.5
  1002.8 2.2 gather_fusion
  1005.0 31.2 %collective-permute-done.5 = f32[256,1536]{1,0:T(8,128)} collective-permute-done((f32[256,1536]{1,0:T(8,128)S(1)}, f32[256,1536]{1,0:T(8,128)}, u32[]{:S(2)}, u32[]{:S(2)}) %collective-permute-start.5) | collective-permute-done | bytes 1572896 | tf_op jit(solution)/shard_map/ppermute | solution.py:146
  1036.2 1.7 add_convert_fusion
  1038.8 2.7 convolution_convert_fusion
  1041.5 6.1 convert_element_type.158
  1047.6 12.2 %all-to-all-start.2 = ((bf16[128,12,1024]{2,1,0:T(8,128)(2,1)}), bf16[128,12,1024]{2,1,0:T(8,128)(2,1)}, u32[]{:S(2)}, u32[]{:S(2)}) async-start(bf16[128,12,1024]{2,1,0:T(8,128)(2,1)} %convert_element_type.158), calls=%async_computation.2 | async-start | bytes 8388608 | tf_op jit(solution)/shard_map/all_to_all | solution.py:154
  1059.8 1.6 constant_dynamic-slice_fusion
  1061.4 100.6 %all-to-all-done.2 = bf16[128,12,1024]{2,1,0:T(8,128)(2,1)} async-done(((bf16[128,12,1024]{2,1,0:T(8,128)(2,1)}), bf16[128,12,1024]{2,1,0:T(8,128)(2,1)}, u32[]{:S(2)}, u32[]{:S(2)}) %all-to-all-start.2) | async-done | bytes 3145760 | tf_op jit(solution)/shard_map/all_to_all | solution.py:154
  1162.0 3.0 convert_reduce_fusion
  (466 shorter events, 246.2 us)
Async XLA Ops:
  7.2 995.7 %copy-start = (bf16[256,1536]{1,0:T(8,128)(2,1)S(1)}, bf16[256,1536]{1,0:T(8,128)(2,1)}, u32[]{:S(2)}) copy-start(bf16[256,1536]{1,0:T(8,128)(2,1)} %param.16) | copy-start | bytes 2359300
  7.2 853.3 %copy-start.3 = (bf16[256,128]{1,0:T(8,128)(2,1)S(1)}, bf16[256,128]{1,0:T(8,128)(2,1)}, u32[]{:S(2)}) copy-start(bf16[256,128]{1,0:T(8,128)(2,1)} %param.11) | copy-start | bytes 196612
  7.2 41.1 %copy-start.5 = (s32[256]{0:T(256)S(1)}, s32[256]{0:T(256)}, u32[]{:S(2)}) copy-start(s32[256]{0:T(256)} %param.13) | copy-start | bytes 3076
  7.2 944.3 %all-gather.3.cloned.1.call-start = ((), (), s32[]{:S(2)}) async-start(), calls=%async_computation.3 | async-start | bytes 4227072 | tf_op jit(solution)/shard_map/all_gather | solution.py:100
  7.2 854.6 %collective-permute-start = (bf16[256,128]{1,0:T(8,128)(2,1)}, bf16[256,128]{1,0:T(8,128)(2,1)S(1)}, u32[]{:S(2)}, u32[]{:S(2)}) collective-permute-start(bf16[256,128]{1,0:T(8,128)(2,1)} %param.12), channel_id=1, source_target_pairs={{0,8},{4,12},{8,16},{12,20},{16,24},{20,28},{24,32},{28,36},{32,40... | collective-permute-start | bytes 196616 | tf_op jit(solution)/shard_map/ppermute | solution.py:35
  9.7 852.2 %collective-permute-start.1 = (bf16[256,128]{1,0:T(8,128)(2,1)}, bf16[256,128]{1,0:T(8,128)(2,1)S(1)}, u32[]{:S(2)}, u32[]{:S(2)}) collective-permute-start(bf16[256,128]{1,0:T(8,128)(2,1)} %param.12), channel_id=1, source_target_pairs={{0,4},{4,8},{8,12},{12,16},{16,20},{20,24},{24,28},{28,32},{32,36}... | collective-permute-start | bytes 196616 | tf_op jit(solution)/shard_map/ppermute | solution.py:35
  12.8 847.6 %collective-permute-start.2 = (bf16[256,128]{1,0:T(8,128)(2,1)}, bf16[256,128]{1,0:T(8,128)(2,1)S(1)}, u32[]{:S(2)}, u32[]{:S(2)}) collective-permute-start(bf16[256,128]{1,0:T(8,128)(2,1)} %param.11), channel_id=1, source_target_pairs={{0,8},{4,12},{8,16},{12,20},{16,24},{20,28},{24,32},{28,36},{32,40... | collective-permute-start | bytes 196616 | tf_op jit(solution)/shard_map/ppermute | solution.py:35
  15.2 845.3 %collective-permute-start.3 = (bf16[256,128]{1,0:T(8,128)(2,1)}, bf16[256,128]{1,0:T(8,128)(2,1)S(1)}, u32[]{:S(2)}, u32[]{:S(2)}) collective-permute-start(bf16[256,128]{1,0:T(8,128)(2,1)} %param.11), channel_id=1, source_target_pairs={{0,4},{4,8},{8,12},{12,16},{16,20},{20,24},{24,28},{28,32},{32,36}... | collective-permute-start | bytes 196616 | tf_op jit(solution)/shard_map/ppermute | solution.py:35
  30.1 874.8 %all-to-all-start = ((s32[128,1,4]{2,1,0:T(1,128)}), s32[128,1,4]{2,1,0:T(1,128)S(1)}, u32[]{:S(2)}, u32[]{:S(2)}) async-start(s32[128,1,4]{2,1,0:T(1,128)} %copy.34), calls=%async_computation | async-start | bytes 131072 | tf_op jit(solution)/shard_map/all_to_all | solution.py:140
  860.5 1.4 copy-start.4
  904.9 43.5 %all-to-all-start.1 = ((bf16[128,4,1024]{2,1,0:T(4,128)(2,1)}), bf16[128,4,1024]{2,1,0:T(4,128)(2,1)S(1)}, u32[]{:S(2)}, u32[]{:S(2)}) async-start(bf16[128,4,1024]{2,1,0:T(4,128)(2,1)} %scatter_fusion.1), calls=%async_computation.1 | async-start | bytes 2097152 | tf_op jit(solution)/shard_map/all_to_all | solution.py:139
  960.6 42.2 %copy-start.6 = (s32[256]{0:T(256)S(1)}, s32[256]{0:T(256)}, u32[]{:S(2)}) copy-start(s32[256]{0:T(256)} %param.17) | copy-start | bytes 3076
  960.6 37.3 %collective-permute-start.4 = (f32[256,1536]{1,0:T(8,128)S(1)}, f32[256,1536]{1,0:T(8,128)S(1)}, u32[]{:S(2)}, u32[]{:S(2)}) collective-permute-start(f32[256,1536]{1,0:T(8,128)S(1)} %fusion.41), channel_id=1, source_target_pairs={{0,1},{1,0},{2,3},{3,2},{4,5},{5,4},{6,7},{7,6},{8,9},{9,8},{10,11... | collective-permute-start | bytes 4718600 | tf_op jit(solution)/shard_map/ppermute | solution.py:146
  998.1 38.0 %collective-permute-start.5 = (f32[256,1536]{1,0:T(8,128)S(1)}, f32[256,1536]{1,0:T(8,128)}, u32[]{:S(2)}, u32[]{:S(2)}) collective-permute-start(f32[256,1536]{1,0:T(8,128)S(1)} %add.90), channel_id=1, source_target_pairs={{0,2},{1,3},{2,0},{3,1},{4,6},{5,7},{6,4},{7,5},{8,10},{9,11},{10,... | collective-permute-start | bytes 4718600 | tf_op jit(solution)/shard_map/ppermute | solution.py:146
  1005.0 33.8 %copy-start.2 = (bf16[256,1536]{1,0:T(8,128)(2,1)S(1)}, bf16[256,1536]{1,0:T(8,128)(2,1)}, u32[]{:S(2)}) copy-start(bf16[256,1536]{1,0:T(8,128)(2,1)} %gather_fusion) | copy-start | bytes 2359300
  1037.9 0.9 copy-start.1
  1047.6 114.4 %all-to-all-start.2 = ((bf16[128,12,1024]{2,1,0:T(8,128)(2,1)}), bf16[128,12,1024]{2,1,0:T(8,128)(2,1)}, u32[]{:S(2)}, u32[]{:S(2)}) async-start(bf16[128,12,1024]{2,1,0:T(8,128)(2,1)} %convert_element_type.158), calls=%async_computation.2 | async-start | bytes 8388608 | tf_op jit(solution)/shard_map/all_to_all | solution.py:154
Sparse Core Ops, SparseCore 0:
  17.5 87.7 all-gather.2
